TPU v7x, 32 devices: a whole 2x2x4 slice. The times are simulated.
32 devices in a mesh: dp: 8 (over y, x, core), hid: 4 (over z).
Axes of the slice: x: 2, y: 2, z: 4, core: 2. Of those that a mesh axis runs over, the one named last changes fastest.
Arguments:
- tokens: bfloat16 [4096, 8192], P('dp', 'hid'), may hold values from -6 to 6
- up_blocks: bfloat16 [7, 64, 128, 1024], P(None, 'hid', 'dp'), may hold values from -0.1875 to 0.1875
- up_left: bfloat16 [8192, 512], P('hid'), may hold values from -0.0625 to 0.0625
- up_right: bfloat16 [512, 65536], P(None, 'hid'), may hold values from -0.25 to 0.25
- down_blocks: bfloat16 [7, 64, 1024, 128], P(None, 'hid', 'dp'), may hold values from -0.0625 to 0.0625
- down_left: bfloat16 [65536, 512], P('hid'), may hold values from -0.0234375 to 0.0234375
- down_right: bfloat16 [512, 8192], P(None, 'hid'), may hold values from -0.25 to 0.25
Outputs:
- mixed: bfloat16 [4096, 8192], P('dp', 'hid')
All inputs are finite; a program needn't handle non-finite values.
Results may differ from a plain program's by a relative error of at most 0.0059.
Values may be sent and summed in bfloat16 or wider, within the bound.
A program may use at most 384 MiB of HBM per device.

v0:
```python
import jax
import jax.numpy as jnp
from jax import lax
from jax.sharding import PartitionSpec as P


def from_partner(block, axis, stride):
    count = lax.axis_size(axis)
    route = []
    for low in range(count):
        high = low | 1 << stride
        if high != low and high < count:
            route += [(low, high), (high, low)]
    return lax.ppermute(block, axis, route)


def swap_blocks(values, block_span, along_axis):
    full_shape = values.shape
    extent = full_shape[along_axis]
    split_shape = (
        full_shape[:along_axis]
        + (extent // (2 * block_span), 2, block_span)
        + full_shape[along_axis + 1 :]
    )
    return jnp.flip(values.reshape(split_shape), along_axis + 1).reshape(full_shape)


def shards(tokens, up_blocks, up_left, up_right, down_blocks, down_left, down_right):
    token_rows = tokens.shape[0]
    local_blocks = up_blocks.shape[1]
    block_size = down_blocks.shape[3]
    term_count = up_blocks.shape[0]
    pieces = tokens.reshape(token_rows, local_blocks, block_size)
    sources = []
    for step_index in range(term_count):
        block_span = 0 if step_index == 0 else 2 ** (step_index - 1)
        if block_span == 0:
            sources.append(pieces)
        elif block_span < local_blocks:
            sources.append(swap_blocks(pieces, block_span, 1))
        else:
            swap_bit = (block_span // local_blocks).bit_length() - 1
            partner_rows = from_partner(tokens, "hid", swap_bit)
            sources.append(partner_rows.reshape(token_rows, local_blocks, block_size))
    stacked = jnp.stack(sources)
    up_full = lax.all_gather(up_blocks, "dp", axis=2, tiled=True)
    hidden_sum = jnp.einsum("tabk,tbkn->abn", stacked, up_full, preferred_element_type=jnp.float32)
    down_full = lax.all_gather(down_blocks, "dp", axis=2, tiled=True)
    rank_up = lax.psum(jnp.dot(tokens, up_left, preferred_element_type=jnp.float32), "hid").astype(
        jnp.bfloat16
    )
    pre_activation = hidden_sum.reshape(
        token_rows, hidden_sum.shape[1] * hidden_sum.shape[2]
    ) + jnp.dot(rank_up, up_right, preferred_element_type=jnp.float32)
    active = jax.nn.gelu(pre_activation, approximate=False).astype(jnp.bfloat16)
    grouped = active.reshape(token_rows, local_blocks, hidden_sum.shape[2])
    contributions = jnp.einsum(
        "abn,tbnk->tabk", grouped, down_full, preferred_element_type=jnp.float32
    )
    out_sum = jnp.zeros((token_rows, local_blocks, block_size), jnp.float32)
    for step_index in range(term_count):
        block_span = 0 if step_index == 0 else 2 ** (step_index - 1)
        if block_span == 0:
            out_sum = contributions[0]
        elif block_span < local_blocks:
            out_sum = out_sum + swap_blocks(contributions[step_index], block_span, 1)
        else:
            swap_bit = (block_span // local_blocks).bit_length() - 1
            out_sum = out_sum + from_partner(contributions[step_index], "hid", swap_bit)
    rank_down = lax.psum(
        jnp.dot(active, down_left, preferred_element_type=jnp.float32), "hid"
    ).astype(jnp.bfloat16)
    result = out_sum.reshape(token_rows, local_blocks * block_size) + jnp.dot(
        rank_down, down_right, preferred_element_type=jnp.float32
    )
    return result.astype(jnp.bfloat16)


def solution(mesh):
    placed = (
        P("dp", "hid"),
        P(None, "hid", "dp", None),
        P("hid", None),
        P(None, "hid"),
        P(None, "hid", "dp", None),
        P("hid", None),
        P(None, "hid"),
    )
    return jax.shard_map(
        shards, mesh=mesh, in_specs=placed, out_specs=P("dp", "hid"), check_vma=False
    )
```

profile of v0, /device:TPU:0, one launch (start us, length us, event | category | flops | bytes accessed | tf_op | source)
XLA Modules:
  0.0 731.4 jit_solution(11911932797676576701)
XLA Ops:
  6.5 4.7 copy.28
  11.3 6.1 copy.31
  17.4 3.9 copy.18
  27.0 4.6 reshape_reshape.12
  31.6 4.5 reshape_reshape.13
  36.0 4.5 reshape_reshape.14
  40.5 3.9 copy.25
  44.4 3.4 copy.19
  51.0 3.4 copy.20
  71.4 4.2 fusion.25
  75.5 5.2 constant_dynamic-update-slice_fusion.6
  89.3 65.1 %all-reduce.2 = bf16[512,512]{1,0:T(8,128)(2,1)} all-reduce(f32[512,512]{1,0:T(8,128)S(1)} %fusion.25), channel_id=1, replica_groups=mesh['dp'=8,'hid'=4] {'hid'}, use_global_device_ids=true, to_apply=%region_0.1 | all-reduce | flops 262144 | bytes 1572864 | tf_op jit(solution)/shard_map/psum | solution.py:49
  154.3 4.1 copy.26
  158.5 3.9 copy.27
  165.8 3.9 constant_dynamic-update-slice_fusion
  169.7 31.9 %convolution_bitcast_fusion = f32[512,16,1024]{2,0,1:T(8,128)} fusion(bf16[7,512,16,128]{3,1,0,2:T(8,128)(2,1)} %constant_dynamic-update-slice_fusion, bf16[7,16,128,1024]{3,2,0,1:T(8,128)(2,1)} %all-gather.3.cloned.1.call-done), kind=kOutput, calls=%fused_computation.21 | convolution fusion | flops 15032385536 | bytes 77594624 | tf_op jit(solution)/shard_map/tabk,tbkn->abn/dot_general | solution.py:47
  201.6 32.2 %copy.29 = f32[512,16,1024]{0,2,1:T(8,128)} copy(f32[512,16,1024]{2,0,1:T(8,128)} %convolution_bitcast_fusion) | data formatting | bytes 67108864 | tf_op jit(solution)/shard_map/tabk,tbkn->abn/transpose | solution.py:47
  233.8 31.3 %copy.30 = f32[512,16384]{1,0:T(8,128)} copy(f32[512,16384]{0,1:T(8,128)} %bitcast.69) | data formatting | bytes 67108864 | tf_op jit(solution)/shard_map/reshape | solution.py:52
  265.1 82.0 %fusion.2 = bf16[512,16384]{1,0:T(8,128)(2,1)S(1)} fusion(f32[512,16384]{1,0:T(8,128)} %copy.30, bf16[512,16384]{1,0:T(8,128)(2,1)} %param.10, bf16[512,512]{1,0:T(8,128)(2,1)S(1)} %copy-done.5), kind=kOutput, calls=%fused_computation.3 | convolution fusion | flops 9143582720 | bytes 67633152 | tf_op jit(solution)/shard_map/dot_general | solution.py:54
  347.1 5.7 copy-done.1
  352.8 12.0 %copy.43 = bf16[64,8,16,1024]{3,2,1,0:T(8,128)(2,1)} copy(bf16[64,8,16,1024]{3,1,2,0:T(8,128)(2,1)S(1)} %bitcast.75) | data formatting | bytes 33554432
  364.8 91.7 %fusion.12 = f32[7,512,16,128]{1,3,0,2:T(8,128)} fusion(bf16[7,16,1024,128]{2,3,0,1:T(8,128)(2,1)} %all-gather.5.cloned.1.call-done, bf16[512,16,1024,1]{2,1,0,3:T(8,128)(2,1)} %bitcast.76), kind=kOutput, calls=%fused_computation.22 | convolution fusion | flops 15032385536 | bytes 75497472 | tf_op jit(solution)/shard_map/abn,tbnk->tabk/dot_general | solution.py:57
  456.6 17.7 %fusion.24 = (f32[1,512,16,128]{1,3,0,2:T(8,128)}, f32[512,16,128]{0,2,1:T(8,128)}, f32[1,512,16,128]{1,3,0,2:T(8,128)}, f32[1,512,16,128]{1,3,0,2:T(8,128)}, f3...) fusion(f32[7,512,16,128]{1,3,0,2:T(8,128)} %fusion.12), kind=kLoop, calls=%fused_computation.43 | loop fusion | bytes 50331648 | tf_op jit(solution)/shard_map/slice | solution.py:66
  476.9 4.8 rev.36
  481.7 4.7 rev.37
  486.4 4.7 rev.38
  491.2 4.8 rev.39
  496.0 18.1 %fusion.26 = f32[512,512]{1,0:T(8,128)} fusion(bf16[512,16384]{1,0:T(8,128)(2,1)} %copy-done.1, bf16[16384,512]{1,0:T(8,128)(2,1)} %param.12), kind=kOutput, calls=%fused_computation.45 | convolution fusion | flops 8589934592 | bytes 34603008 | tf_op jit(solution)/shard_map/dot_general | solution.py:71
  514.1 183.0 %all-reduce.3 = bf16[512,512]{1,0:T(8,128)(2,1)S(1)} all-reduce(f32[512,512]{1,0:T(8,128)} %fusion.26), channel_id=1, replica_groups=mesh['dp'=8,'hid'=4] {'hid'}, use_global_device_ids=true, to_apply=%region_1.2 | all-reduce | flops 262144 | bytes 1572864 | tf_op jit(solution)/shard_map/psum | solution.py:70
  700.2 13.4 %fusion.20 = f32[512,16,128]{0,2,1:T(8,128)} fusion(f32[512,16,128]{0,2,1:T(8,128)} %collective-permute-done.3, f32[512,16,128]{0,2,1:T(8,128)} %collective-permute-done.2, f32[7,512,16,128]{1,3,0,2:T(8,128)} %fusion.12, f32[512,1,2,8,128]{0,4,3,2,1:T(8,128)} %rev.39, f32[512,2,2,4,128]{0,4,3,2,1:T(8,128)} %rev.38, f32[512,4,2,2,128]{0,4,3,2,1:T(8,128)} %rev.37, ...), kind=kLoop, calls=%fused_computation.31 | loop fusion | flops 6291456 | bytes 33554432 | tf_op jit(solution)/shard_map/add | solution.py:69
  713.6 5.4 copy.35
  719.0 5.4 add_convert_fusion
  (38 shorter events, 43.6 us)
Async XLA Ops:
  6.5 690.5 %copy-start = (bf16[512,2048]{1,0:T(8,128)(2,1)S(1)}, bf16[512,2048]{1,0:T(8,128)(2,1)}, u32[]{:S(2)}) copy-start(bf16[512,2048]{1,0:T(8,128)(2,1)} %param.13) | copy-start | bytes 6291460
  6.5 163.1 %all-gather.3.cloned.1.call-start = ((), (), s32[]{:S(2)}) async-start(), calls=%async_computation | async-start | bytes 33030144 | tf_op jit(solution)/shard_map/all_gather | solution.py:46
  11.2 353.6 %all-gather.5.cloned.1.call-start = ((), (), s32[]{:S(2)}) async-start(), calls=%async_computation.1 | async-start | bytes 33030144 | tf_op jit(solution)/shard_map/all_gather | solution.py:48
  21.3 133.0 %collective-permute-start = (bf16[512,2048]{0,1:T(8,128)(2,1)}, bf16[512,2048]{0,1:T(8,128)(2,1)}, u32[]{:S(2)}, u32[]{:S(2)}) collective-permute-start(bf16[512,2048]{0,1:T(8,128)(2,1)} %copy.18), channel_id=1, source_target_pairs={{0,1},{1,0},{2,3},{3,2},{4,5},{5,4},{6,7},{7,6},{8,9},{9,8},{10,11... | collective-permute-start | bytes 6291464 | tf_op jit(solution)/shard_map/ppermute | solution.py:14
  24.4 134.1 %collective-permute-start.1 = (bf16[512,2048]{0,1:T(8,128)(2,1)}, bf16[512,2048]{0,1:T(8,128)(2,1)}, u32[]{:S(2)}, u32[]{:S(2)}) collective-permute-start(bf16[512,2048]{0,1:T(8,128)(2,1)} %copy.18), channel_id=1, source_target_pairs={{0,2},{2,0},{1,3},{3,1},{4,6},{6,4},{5,7},{7,5},{8,10},{10,8},{9,1... | collective-permute-start | bytes 6291464 | tf_op jit(solution)/shard_map/ppermute | solution.py:14
  71.3 12.8 %copy-start.2 = (bf16[512,4,2,2,128]{4,0,3,2,1:T(8,128)(2,1)S(1)}, bf16[512,4,2,2,128]{4,0,3,2,1:T(8,128)(2,1)}, u32[]{:S(2)}) copy-start(bf16[512,4,2,2,128]{4,0,3,2,1:T(8,128)(2,1)} %rev.33) | copy-start | bytes 6291460
  71.4 14.5 %copy-start.3 = (bf16[512,2,2,4,128]{4,0,3,2,1:T(8,128)(2,1)S(1)}, bf16[512,2,2,4,128]{4,0,3,2,1:T(8,128)(2,1)}, u32[]{:S(2)}) copy-start(bf16[512,2,2,4,128]{4,0,3,2,1:T(8,128)(2,1)} %rev.34) | copy-start | bytes 6291460
  71.4 16.2 %copy-start.4 = (bf16[512,1,2,8,128]{4,0,3,2,1:T(8,128)(2,1)S(1)}, bf16[512,1,2,8,128]{4,0,3,2,1:T(8,128)(2,1)}, u32[]{:S(2)}) copy-start(bf16[512,1,2,8,128]{4,0,3,2,1:T(8,128)(2,1)} %rev.35) | copy-start | bytes 6291460
  233.8 31.3 %copy-start.5 = (bf16[512,512]{1,0:T(8,128)(2,1)S(1)}, bf16[512,512]{1,0:T(8,128)(2,1)}, u32[]{:S(2)}) copy-start(bf16[512,512]{1,0:T(8,128)(2,1)} %all-reduce.2) | copy-start | bytes 1572868
  347.1 5.7 copy-start.1
  474.3 226.0 %collective-permute-start.2 = (f32[512,16,128]{0,2,1:T(8,128)}, f32[512,16,128]{0,2,1:T(8,128)}, u32[]{:S(2)}, u32[]{:S(2)}) collective-permute-start(f32[512,16,128]{0,2,1:T(8,128)} %get-tuple-element.10), channel_id=1, source_target_pairs={{0,1},{1,0},{2,3},{3,2},{4,5},{5,4},{6,7},{7,6},{8,9},{9,8},{10,11... | collective-permute-start | bytes 12582920 | tf_op jit(solution)/shard_map/ppermute | solution.py:14
  474.5 225.7 %collective-permute-start.3 = (f32[512,16,128]{0,2,1:T(8,128)}, f32[512,16,128]{0,2,1:T(8,128)}, u32[]{:S(2)}, u32[]{:S(2)}) collective-permute-start(f32[512,16,128]{0,2,1:T(8,128)} %get-tuple-element.6), channel_id=1, source_target_pairs={{0,2},{2,0},{1,3},{3,1},{4,6},{6,4},{5,7},{7,5},{8,10},{10,8},{9,1... | collective-permute-start | bytes 12582920 | tf_op jit(solution)/shard_map/ppermute | solution.py:14
Sparse Core Ops, SparseCore 0:
  11.3 145.7 all-gather.2
  159.0 148.8 all-gather.4
where the time goes:
time: 740 us; the launch traced here: 731 us
  blocking collectives  248 us (34%)
  matrix products  231 us (31%)
  local copies, waits for them, and re-layouts  211 us (29%)
  other arithmetic  18.8 us (3%)
  between operations  13.7 us (2%)
  starting transfers between devices  8.36 us (1%)
    psum x1, blocking collectives, shards(): lax.psum(jnp.dot(active, down_left, preferred_element_type=jnp.float32),...  183 us
    dot_general x1, matrix products, shards(): jnp.einsum('abn,tbnk->tabk', grouped, down_full, preferred_element_type=j...  91.7 us
    dot_general x1, matrix products, shards(): jnp.dot(rank_up, up_right, preferred_element_type=jnp.float32)  82 us
    psum x1, blocking collectives, shards(): lax.psum(jnp.dot(tokens, up_left, preferred_element_type=jnp.float32), 'h...  65.1 us
    unnamed x23, local copies, waits for them, and re-layouts  51.8 us
    transpose x1, local copies, waits for them, and re-layouts, shards(): jnp.einsum('tabk,tbkn->abn', stacked, up_full, preferred_element_type=jnp...  32.2 us
    dot_general x1, matrix products, shards(): jnp.einsum('tabk,tbkn->abn', stacked, up_full, preferred_element_type=jnp...  31.9 us
    rev x8, local copies, waits for them, and re-layouts, swap_blocks(): jnp.flip(values.reshape(split_shape), along_axis + 1).reshape(full_shape)  31.6 us
  transfers between devices with their start and end apart: 6, of which 0 were waited for; matrix products, arithmetic and copies ran while one was open for 43% of the time, Pallas kernels for 0%

commit v1 on v0

--- a/solution.py
+++ b/solution.py
@@ -46,9 +46,9 @@
     up_full = lax.all_gather(up_blocks, "dp", axis=2, tiled=True)
     hidden_sum = jnp.einsum("tabk,tbkn->abn", stacked, up_full, preferred_element_type=jnp.float32)
     down_full = lax.all_gather(down_blocks, "dp", axis=2, tiled=True)
-    rank_up = lax.psum(jnp.dot(tokens, up_left, preferred_element_type=jnp.float32), "hid").astype(
-        jnp.bfloat16
-    )
+    rank_up = jnp.sum(
+        lax.all_gather(jnp.dot(tokens, up_left, preferred_element_type=jnp.float32), "hid"), axis=0
+    ).astype(jnp.bfloat16)
     pre_activation = hidden_sum.reshape(
         token_rows, hidden_sum.shape[1] * hidden_sum.shape[2]
     ) + jnp.dot(rank_up, up_right, preferred_element_type=jnp.float32)

time: 740 us -> 900 us (1.22)
  waiting for transfers between devices: 0.05 us -> 206 us
  blocking collectives: 248 us -> 182 us
  local copies, waits for them, and re-layouts: 211 us -> 225 us
    all_gather x1, waiting for transfers between devices: 0.01 us -> 113 us  [shards(): up_full = lax.all_gather(up_blocks, 'dp', axis=2, tiled=True)]
    ppermute x4, waiting for transfers between devices: 0.01 us -> 93.3 us  [from_partner(): return lax.ppermute(block, axis, route)]
    psum x1 -> x0, blocking collectives: 65.1 us -> none  [shards(): lax.psum(jnp.dot(tokens, up_left, preferred_element_type=jnp.float32), 'h...]
    reshape x1, local copies, waits for them, and re-layouts: 31.3 us -> 45.3 us  [shards(): hidden_sum.reshape(token_rows, hidden_sum.shape[1] * hidden_sum.shape[2])]
    unnamed x23 -> x19, local copies, waits for them, and re-layouts: 51.8 us -> 51.2 us
  transfers between devices with their start and end apart: 6 -> 7, of which waited for: 0 -> 2; matrix products, arithmetic and copies ran while one was open for 43% -> 37% of each run, Pallas kernels for 0% -> 0%
where the time goes in v1:
time: 900 us; the launch traced here: 888 us
  matrix products  231 us (26%)
  local copies, waits for them, and re-layouts  225 us (25%)
  waiting for transfers between devices  206 us (23%)
  blocking collectives  182 us (20%)
  other arithmetic  21.5 us (2%)
  between operations  13.6 us (2%)
  starting transfers between devices  9.33 us (1%)
    psum x1, blocking collectives, shards(): lax.psum(jnp.dot(active, down_left, preferred_element_type=jnp.float32),...  182 us
    all_gather x1, waiting for transfers between devices, shards(): up_full = lax.all_gather(up_blocks, 'dp', axis=2, tiled=True)  113 us
    ppermute x4, waiting for transfers between devices, from_partner(): return lax.ppermute(block, axis, route)  93.3 us
    dot_general x1, matrix products, shards(): jnp.einsum('abn,tbnk->tabk', grouped, down_full, preferred_element_type=j...  91.5 us
    dot_general x1, matrix products, shards(): jnp.dot(rank_up, up_right, preferred_element_type=jnp.float32)  82 us
    unnamed x19, local copies, waits for them, and re-layouts  51.2 us
    reshape x1, local copies, waits for them, and re-layouts, shards(): hidden_sum.reshape(token_rows, hidden_sum.shape[1] * hidden_sum.shape[2])  45.3 us
    transpose x1, local copies, waits for them, and re-layouts, shards(): jnp.einsum('tabk,tbkn->abn', stacked, up_full, preferred_element_type=jnp...  32.4 us
  transfers between devices with their start and end apart: 7, of which 2 were waited for; matrix products, arithmetic and copies ran while one was open for 37% of the time, Pallas kernels for 0%

profile of v1, /device:TPU:0, one launch (start us, length us, event | category | flops | bytes accessed | tf_op | source)
XLA Modules:
  0.0 888.3 jit_solution(6299470307812568661)
XLA Ops:
  6.5 4.6 fusion.25
  11.2 4.5 copy.28
  15.8 6.1 copy.31
  22.0 4.0 copy.18
  31.6 4.5 reshape_reshape.12
  36.1 4.4 reshape_reshape.13
  40.5 4.5 reshape_reshape.14
  45.0 3.9 copy.25
  48.9 3.5 copy.19
  55.4 3.5 copy.20
  83.8 5.2 copy-done.3
  89.1 93.3 %collective-permute-done = bf16[512,2048]{0,1:T(8,128)(2,1)} collective-permute-done((bf16[512,2048]{0,1:T(8,128)(2,1)}, bf16[512,2048]{0,1:T(8,128)(2,1)}, u32[]{:S(2)}, u32[]{:S(2)}) %collective-permute-start) | collective-permute-done | bytes 2097184 | tf_op jit(solution)/shard_map/ppermute | solution.py:14
  182.4 4.2 copy.26
  186.6 3.9 copy.27
  200.1 112.8 %all-gather.5.cloned.1.call-done = bf16[7,16,128,1024]{3,2,0,1:T(8,128)(2,1)} async-done(((bf16[7,16,16,1024]{3,2,0,1:T(8,128)(2,1)}), bf16[7,16,128,1024]{3,2,0,1:T(8,128)(2,1)}) %all-gather.5.cloned.1.call-update) | async-done | bytes 29360144 | tf_op jit(solution)/shard_map/all_gather | solution.py:46
  312.9 31.9 %convolution_bitcast_fusion = f32[512,16,1024]{2,0,1:T(8,128)} fusion(bf16[7,512,16,128]{3,1,0,2:T(8,128)(2,1)} %constant_dynamic-update-slice_fusion, bf16[7,16,128,1024]{3,2,0,1:T(8,128)(2,1)} %all-gather.5.cloned.1.call-done), kind=kOutput, calls=%fused_computation.21 | convolution fusion | flops 15032385536 | bytes 77594624 | tf_op jit(solution)/shard_map/tabk,tbkn->abn/dot_general | solution.py:47
  344.9 32.4 %copy.29 = f32[512,16,1024]{0,2,1:T(8,128)} copy(f32[512,16,1024]{2,0,1:T(8,128)} %convolution_bitcast_fusion) | data formatting | bytes 67108864 | tf_op jit(solution)/shard_map/tabk,tbkn->abn/transpose | solution.py:47
  377.3 45.3 %copy.30 = f32[512,16384]{1,0:T(8,128)} copy(f32[512,16384]{0,1:T(8,128)} %bitcast.70) | data formatting | bytes 67108864 | tf_op jit(solution)/shard_map/reshape | solution.py:52
  422.6 82.0 %fusion.2 = bf16[512,16384]{1,0:T(8,128)(2,1)S(1)} fusion(f32[512,16384]{1,0:T(8,128)} %copy.30, bf16[512,16384]{1,0:T(8,128)(2,1)} %param.10, bf16[512,512]{1,0:T(8,128)(2,1)S(1)} %reduce_sum.9), kind=kOutput, calls=%fused_computation.3 | convolution fusion | flops 9143582720 | bytes 67633152 | tf_op jit(solution)/shard_map/dot_general | solution.py:54
  504.6 5.7 copy-done.1
  510.3 12.0 %copy.43 = bf16[64,8,16,1024]{3,2,1,0:T(8,128)(2,1)} copy(bf16[64,8,16,1024]{3,1,2,0:T(8,128)(2,1)S(1)} %bitcast.76) | data formatting | bytes 33554432
  522.3 91.5 %fusion.12 = f32[7,512,16,128]{1,3,0,2:T(8,128)} fusion(bf16[7,16,1024,128]{2,3,0,1:T(8,128)(2,1)} %all-gather.7.cloned.1.call-done, bf16[512,16,1024,1]{2,1,0,3:T(8,128)(2,1)} %bitcast.77), kind=kOutput, calls=%fused_computation.22 | convolution fusion | flops 15032385536 | bytes 75497472 | tf_op jit(solution)/shard_map/abn,tbnk->tabk/dot_general | solution.py:57
  613.8 17.7 %fusion.24 = (f32[1,512,16,128]{1,3,0,2:T(8,128)}, f32[512,16,128]{0,2,1:T(8,128)}, f32[1,512,16,128]{1,3,0,2:T(8,128)}, f32[1,512,16,128]{1,3,0,2:T(8,128)}, f3...) fusion(f32[7,512,16,128]{1,3,0,2:T(8,128)} %fusion.12), kind=kLoop, calls=%fused_computation.43 | loop fusion | bytes 50331648 | tf_op jit(solution)/shard_map/slice | solution.py:66
  635.2 4.8 rev.36
  639.9 4.7 rev.37
  644.6 4.7 rev.38
  649.4 4.8 rev.39
  654.2 18.1 %fusion.26 = f32[512,512]{1,0:T(8,128)} fusion(bf16[512,16384]{1,0:T(8,128)(2,1)} %copy-done.1, bf16[16384,512]{1,0:T(8,128)(2,1)} %param.12), kind=kOutput, calls=%fused_computation.45 | convolution fusion | flops 8589934592 | bytes 34603008 | tf_op jit(solution)/shard_map/dot_general | solution.py:71
  672.3 181.7 %all-reduce.1 = bf16[512,512]{1,0:T(8,128)(2,1)S(1)} all-reduce(f32[512,512]{1,0:T(8,128)} %fusion.26), channel_id=1, replica_groups=mesh['dp'=8,'hid'=4] {'hid'}, use_global_device_ids=true, to_apply=%region_1.2 | all-reduce | flops 262144 | bytes 1572864 | tf_op jit(solution)/shard_map/psum | solution.py:70
  857.2 13.4 %fusion.20 = f32[512,16,128]{0,2,1:T(8,128)} fusion(f32[512,16,128]{0,2,1:T(8,128)} %collective-permute-done.3, f32[512,16,128]{0,2,1:T(8,128)} %collective-permute-done.2, f32[7,512,16,128]{1,3,0,2:T(8,128)} %fusion.12, f32[512,1,2,8,128]{0,4,3,2,1:T(8,128)} %rev.39, f32[512,2,2,4,128]{0,4,3,2,1:T(8,128)} %rev.38, f32[512,4,2,2,128]{0,4,3,2,1:T(8,128)} %rev.37, ...), kind=kLoop, calls=%fused_computation.31 | loop fusion | flops 6291456 | bytes 33554432 | tf_op jit(solution)/shard_map/add | solution.py:69
  870.5 5.4 copy.35
  875.9 5.4 add_convert_fusion
  (37 shorter events, 50.1 us)
Async XLA Ops:
  6.5 847.4 %copy-start = (bf16[512,2048]{1,0:T(8,128)(2,1)S(1)}, bf16[512,2048]{1,0:T(8,128)(2,1)}, u32[]{:S(2)}) copy-start(bf16[512,2048]{1,0:T(8,128)(2,1)} %param.13) | copy-start | bytes 6291460
  6.5 190.8 %all-gather.9.cloned.1.call-start = ((), (), s32[]{:S(2)}) async-start(), calls=%async_computation.2 | async-start | bytes 5242880 | tf_op jit(solution)/shard_map/all_gather | solution.py:50
  11.2 301.8 %all-gather.5.cloned.1.call-start = ((), (), s32[]{:S(2)}) async-start(), calls=%async_computation | async-start | bytes 33030144 | tf_op jit(solution)/shard_map/all_gather | solution.py:46
  15.8 506.5 %all-gather.7.cloned.1.call-start = ((), (), s32[]{:S(2)}) async-start(), calls=%async_computation.1 | async-start | bytes 33030144 | tf_op jit(solution)/shard_map/all_gather | solution.py:48
  26.0 156.4 %collective-permute-start = (bf16[512,2048]{0,1:T(8,128)(2,1)}, bf16[512,2048]{0,1:T(8,128)(2,1)}, u32[]{:S(2)}, u32[]{:S(2)}) collective-permute-start(bf16[512,2048]{0,1:T(8,128)(2,1)} %copy.18), channel_id=1, source_target_pairs={{0,1},{1,0},{2,3},{3,2},{4,5},{5,4},{6,7},{7,6},{8,9},{9,8},{10,11... | collective-permute-start | bytes 6291464 | tf_op jit(solution)/shard_map/ppermute | solution.py:14
  29.0 157.6 %collective-permute-start.1 = (bf16[512,2048]{0,1:T(8,128)(2,1)}, bf16[512,2048]{0,1:T(8,128)(2,1)}, u32[]{:S(2)}, u32[]{:S(2)}) collective-permute-start(bf16[512,2048]{0,1:T(8,128)(2,1)} %copy.18), channel_id=1, source_target_pairs={{0,2},{2,0},{1,3},{3,1},{4,6},{6,4},{5,7},{7,5},{8,10},{10,8},{9,1... | collective-permute-start | bytes 6291464 | tf_op jit(solution)/shard_map/ppermute | solution.py:14
  75.8 7.7 copy-start.2
  83.8 5.3 copy-start.3
  504.6 5.7 copy-start.1
  631.5 225.7 %collective-permute-start.2 = (f32[512,16,128]{0,2,1:T(8,128)}, f32[512,16,128]{0,2,1:T(8,128)}, u32[]{:S(2)}, u32[]{:S(2)}) collective-permute-start(f32[512,16,128]{0,2,1:T(8,128)} %get-tuple-element.10), channel_id=1, source_target_pairs={{0,1},{1,0},{2,3},{3,2},{4,5},{5,4},{6,7},{7,6},{8,9},{9,8},{10,11... | collective-permute-start | bytes 12582920 | tf_op jit(solution)/shard_map/ppermute | solution.py:14
  632.8 224.4 %collective-permute-start.3 = (f32[512,16,128]{0,2,1:T(8,128)}, f32[512,16,128]{0,2,1:T(8,128)}, u32[]{:S(2)}, u32[]{:S(2)}) collective-permute-start(f32[512,16,128]{0,2,1:T(8,128)} %get-tuple-element.6), channel_id=1, source_target_pairs={{0,2},{2,0},{1,3},{3,1},{4,6},{6,4},{5,7},{7,5},{8,10},{10,8},{9,1... | collective-permute-start | bytes 12582920 | tf_op jit(solution)/shard_map/ppermute | solution.py:14
Sparse Core Ops, SparseCore 0:
  11.3 155.9 all-gather.8
  169.2 143.7 all-gather.4
  314.8 148.8 all-gather.6
